TPU v7x, 32 devices: a whole 2x2x4 slice. The times are simulated.
32 devices in a mesh: dp: 4 (over x, core), tm: 8 (over z, y).
Axes of the slice: x: 2, y: 2, z: 4, core: 2. Of those that a mesh axis runs over, the one named last changes fastest.
Arguments:
- latent: float32 [4, 64, 4096], P('dp', None, 'tm'), may hold values from -40 to 40
- target: float32 [4, 8192], P('dp', 'tm'), may hold values from -20 to 20
- up_kernel: float32 [4, 32, 64], replicated, may hold values from -0.5 to 0.5
- inner_kernel: float32 [3, 16, 32], replicated, may hold values from -0.625 to 0.625
- outer_kernel: float32 [32, 16], replicated, may hold values from -1.5 to 1.5
- out_kernel: float32 [7, 32], replicated, may hold values from -0.375 to 0.375
Outputs:
- latent_grad: float32 [4, 64, 4096], P('dp', None, 'tm')
- up_update: float32 [4, 32, 64], replicated
- inner_update: float32 [3, 16, 32], replicated
- outer_update: float32 [32, 16], replicated
- out_update: float32 [7, 32], replicated
All inputs are finite; a program needn't handle non-finite values.
Results may differ from a plain program's by a relative error of at most 0.0003.
Values sent between devices are 32-bit elements; how exact they have to be, the bound alone decides.
No kernel may reach another device: no remote copies, remote signals or barrier semaphores. Data moves between devices by JAX's collectives and lax.ppermute only.
A program may use at most 64 MiB of HBM per device.

v0:
```python
import jax
import jax.numpy as jnp
from jax import lax
from jax.sharding import PartitionSpec as P

MELS = 64
WIN_COARSE = 1024
WIN_FINE = 256
LOSS_WEIGHTS = (0.25, 0.5, 0.5)


def padded_2(cells, sides, width):
    for axis, dim in sides:
        count = lax.axis_size(axis)
        ends = count - 1
        head = lax.slice_in_dim(cells, 0, width, axis=dim)
        tail = lax.slice_in_dim(cells, cells.shape[dim] - width, cells.shape[dim], axis=dim)
        cells = jnp.concatenate(
            [
                lax.ppermute(tail, axis, [(i, (i + 1) % count) for i in range(ends)]),
                cells,
                lax.ppermute(head, axis, [((i + 1) % count, i) for i in range(ends)]),
            ],
            axis=dim,
        )
    return cells


def from_behind(x, axis, by):
    peers = lax.axis_size(axis)
    pairs = [(i, i + by) for i in range(peers) if 0 <= i + by < peers]
    return lax.ppermute(x, axis, pairs)


def product(form, left, right):
    return jnp.einsum(
        form, left, right, precision=lax.Precision.HIGHEST, preferred_element_type=jnp.float32
    )


def mel_bank(window, mel_count):
    half_window = window // 2
    top_mel = 2595.0 * jnp.log10(1.0 + 12000.0 / 700.0)
    points = (jnp.arange(mel_count + 1, dtype=jnp.float32) + 1.0) / (mel_count + 2.0) * top_mel
    centers = 700.0 * (jnp.power(10.0, points / 2595.0) - 1.0) / 12000.0 * half_window
    spacing = jnp.maximum(centers[1:] - centers[:-1], 1.0)
    places = jnp.arange(half_window, dtype=jnp.float32)[:, None]
    return jnp.maximum(0.0, 1.0 - jnp.abs(places - centers[None, :mel_count]) / spacing[None, :])


def dft_table(window):
    half_window = window // 2
    sample = jnp.arange(window, dtype=jnp.int32)[:, None]
    freq_index = jnp.arange(half_window, dtype=jnp.int32)[None, :]
    angles = (sample * freq_index % window).astype(jnp.float32) * (2.0 * jnp.pi / window)
    hann_taper = 0.5 - 0.5 * jnp.cos(sample.astype(jnp.float32) * (2.0 * jnp.pi / window))
    return jnp.concatenate([hann_taper * jnp.cos(angles), -hann_taper * jnp.sin(angles)], axis=1)


def framed(signal, window, frame_count):
    hop_size = window // 4
    blocks = signal.reshape(signal.shape[:-1] + (frame_count + 3, hop_size))
    return jnp.concatenate(
        [blocks[..., offset : offset + frame_count, :] for offset in range(4)], axis=-1
    )


def mel_energy(signal, window, frame_count):
    frames = framed(signal, window, frame_count)
    spectra = product("...nf,fk->...nk", frames, dft_table(window))
    half_window = window // 2
    energy = spectra[..., :half_window] ** 2 + spectra[..., half_window:] ** 2
    return product("...nk,km->...nm", energy, mel_bank(window, MELS))


def spectral_loss(signal, target_mel, window, frame_count):
    level = jnp.sqrt(mel_energy(signal, window, frame_count) + 1.0)
    return jnp.sum((level - jnp.sqrt(target_mel + 1.0)) ** 2)


def elu_slope(values):
    return jnp.where(values > 0, 1.0, jnp.exp(jnp.minimum(values, 0.0)))


def apply_mask(values, mask):
    return values * mask


def upsample_forward(values, kernel, stride, previous):
    lagged = jnp.concatenate([previous, values[:, :, :-1]], axis=2)
    phases = product("pij,bjm->bimp", kernel[:stride], values) + product(
        "pij,bjm->bimp", kernel[stride:], lagged
    )
    return (phases.reshape(phases.shape[0], phases.shape[1], -1), lagged)


def taps_forward(padded, kernel, length):
    summed = product("oi,bil->bol", kernel[0], padded[:, :, :length])
    for offset in range(1, kernel.shape[0]):
        summed = summed + product(
            "oi,bil->bol", kernel[offset], padded[:, :, offset : offset + length]
        )
    return summed


def decode_forward(activated, weights, movers, clip_mask):
    up_kernel, inner_kernel, outer_kernel, out_kernel = weights
    lend_frame, border_inner, border_output = movers
    upper, lagged = upsample_forward(activated, up_kernel, 2, lend_frame(activated[:, :, -1:]))
    upper = apply_mask(upper, clip_mask)
    padded_inner = border_inner(jax.nn.elu(upper))
    inner_out = taps_forward(padded_inner, inner_kernel, upper.shape[2])
    hidden = jax.nn.elu(inner_out)
    mixed = apply_mask(upper + product("oi,bil->bol", outer_kernel, hidden), clip_mask)
    padded_output = border_output(jax.nn.elu(mixed))
    waveform = taps_forward(padded_output, out_kernel[:, None, :], upper.shape[2])[:, 0, :]
    return (waveform, (upper, lagged, padded_inner, inner_out, hidden, mixed, padded_output))


def taps_backward(grad_out, padded, kernel, length, keep):
    tap_count = kernel.shape[0]
    row_grad = apply_mask(grad_out, keep)
    kernel_rows = jnp.stack(
        [
            product("nbol,bil->nboi", row_grad, padded[:, :, offset : offset + length])
            for offset in range(tap_count)
        ],
        axis=2,
    )
    spread = jnp.zeros(grad_out.shape[:2] + (kernel.shape[2], length + tap_count - 1), jnp.float32)
    for offset in range(tap_count):
        moved = product("oi,nbol->nbil", kernel[offset], grad_out)
        spread = spread + jnp.pad(moved, ((0, 0), (0, 0), (0, 0), (offset, tap_count - 1 - offset)))
    return (kernel_rows, spread)


def rims_backward(spread, rim_width):
    interior = spread[..., rim_width:-rim_width]
    return interior


def residual_backward(
    grad_mixed, upper, padded, inner_out, hidden, inner_kernel, outer_kernel, keep
):
    length = upper.shape[-1]
    outer_rows = product("nbol,bil->nboi", apply_mask(grad_mixed, keep), hidden)
    grad_inner = product("oi,nbol->nbil", outer_kernel, grad_mixed) * elu_slope(inner_out)
    inner_rows, spread = taps_backward(grad_inner, padded, inner_kernel, length, keep)
    grad_rectified = rims_backward(spread, 1)
    return (grad_mixed + grad_rectified * elu_slope(upper), inner_rows, outer_rows)


def upsample_backward(grad_upper, values, lagged, kernel, stride, keep):
    phase_shape = grad_upper.shape[:3] + (values.shape[-1], stride)
    grad_phase = grad_upper.reshape(phase_shape)
    row_phase = apply_mask(grad_upper, keep).reshape(phase_shape)
    first_rows = product("nbimp,bjm->nbpij", row_phase, values)
    second_rows = product("nbimp,bjm->nbpij", row_phase, lagged)
    grad_values = product("pij,nbimp->nbjm", kernel[:stride], grad_phase)
    grad_lagged = product("pij,nbimp->nbjm", kernel[stride:], grad_phase)
    arrived = jnp.zeros_like(grad_lagged[..., :1])
    grad_values = grad_values + jnp.concatenate([grad_lagged[..., 1:], arrived], axis=-1)
    return (grad_values, jnp.concatenate([first_rows, second_rows], axis=2))


def local(latent, target, up_kernel, inner_kernel, outer_kernel, out_kernel):
    weights = (up_kernel, inner_kernel, outer_kernel, out_kernel)
    clips_here = target.shape[0]
    samples = target.shape[1]
    frames_here = latent.shape[2]
    latent_in = padded_2(latent, (("tm", 2),), 4)
    start_frame = 4
    margin = 8

    def lend_frame(edge):
        return jnp.zeros_like(edge)

    def border_inner(values):
        return jnp.pad(values, ((0, 0), (0, 0), (1, 1)))

    def border_output(values):
        return jnp.pad(values, ((0, 0), (0, 0), (3, 3)))

    shard_index = lax.axis_index("tm")
    shard_total = lax.axis_size("tm")
    wide_length = samples + 2 * margin
    local_places = jnp.arange(wide_length, dtype=jnp.int32)
    clip_places = samples * shard_index - margin + local_places
    clip_mask = ((clip_places >= 0) & (clip_places < samples * shard_total)).astype(jnp.float32)
    keep_rows = ((local_places >= margin) & (local_places < margin + samples)).astype(jnp.float32)
    activated = jax.nn.elu(latent_in)
    wave_all, saved = decode_forward(
        activated, weights, (lend_frame, border_inner, border_output), clip_mask
    )
    upper, lagged, padded_inner, inner_out, hidden, mixed, padded_output = saved
    waveform = wave_all[:, margin : margin + samples]
    tail_length = 3 * WIN_COARSE // 4
    wave_next, target_next = from_behind(
        (waveform[:, :tail_length], target[:, :tail_length]), "tm", -1
    )
    long_wave = jnp.concatenate([waveform, wave_next], axis=1)
    long_target = jnp.concatenate([target, target_next], axis=1)
    gradients = [2.0 * (waveform - target)]
    tails = []
    for window in (WIN_COARSE, WIN_FINE):
        hop_size = window // 4
        frame_count = samples // hop_size
        span = samples + 3 * hop_size
        target_mel = mel_energy(long_target[:, :span], window, frame_count)

        def scale_loss(signal):
            return spectral_loss(signal, target_mel, window, frame_count)

        local_grad = jax.grad(scale_loss)(long_wave[:, :span])
        gradients.append(local_grad[:, :samples])
        tails.append(jnp.pad(local_grad[:, samples:], ((0, 0), (0, tail_length - 3 * hop_size))))
    coarse_in, fine_in = from_behind((tails[0], tails[1]), "tm", 1)
    gradients[1] = gradients[1] + jnp.pad(coarse_in, ((0, 0), (0, samples - tail_length)))
    gradients[2] = gradients[2] + jnp.pad(fine_in, ((0, 0), (0, samples - tail_length)))
    squares = jnp.stack([jnp.sum(member * member, axis=1) for member in gradients], axis=1)
    squares = lax.psum(squares, "tm")
    total_samples = samples * lax.axis_size("tm")
    grad_scale = jnp.asarray(LOSS_WEIGHTS, jnp.float32)[None, :] / jnp.sqrt(
        squares / total_samples + 1e-06
    )
    streams = (
        gradients[0] * grad_scale[:, 0, None]
        + gradients[1] * grad_scale[:, 1, None]
        + gradients[2] * grad_scale[:, 2, None]
    )[None]
    row_weights = jnp.ones((1, clips_here), jnp.float32)
    streams_wide = padded_2(streams, (("tm", 2),), 8)
    wave_length = mixed.shape[2]
    out_taps = out_kernel[:, None, :]
    kernel_rows_out, spread_out = taps_backward(
        streams_wide[:, :, None, :], padded_output, out_taps, wave_length, keep_rows
    )
    out_rows = kernel_rows_out[:, :, :, 0, :]
    grad_final = rims_backward(spread_out, 3)
    grad_mixed = apply_mask(grad_final * elu_slope(mixed), clip_mask)
    grad_upper, inner_rows, outer_rows = residual_backward(
        grad_mixed, upper, padded_inner, inner_out, hidden, inner_kernel, outer_kernel, keep_rows
    )
    grad_activated, up_rows = upsample_backward(
        apply_mask(grad_upper, clip_mask), activated, lagged, up_kernel, 2, keep_rows
    )
    grad_latent_rows = grad_activated[..., start_frame : start_frame + frames_here] * elu_slope(
        latent
    )
    latent_grad = product("nb,nbcm->bcm", row_weights, grad_latent_rows)
    local_totals = [
        product("nb,nb...->...", row_weights, member)
        for member in (up_rows, inner_rows, outer_rows, out_rows)
    ]
    param_count = sum((member.size for member in local_totals))
    summed = lax.psum(
        (local_totals[0], local_totals[1], local_totals[2], local_totals[3]), ("dp", "tm")
    )
    squares_all = sum((jnp.sum(member * member) for member in summed))
    factor = jnp.minimum(1.0, 1.0 / jnp.sqrt(squares_all / param_count + 1e-06))
    updates = [member * factor for member in summed]
    return (latent_grad, updates[0], updates[1], updates[2], updates[3])


def solution(mesh):
    placed = (P("dp", None, "tm"), P("dp", "tm"), P(), P(), P(), P())
    return jax.shard_map(
        local,
        mesh=mesh,
        in_specs=placed,
        out_specs=(P("dp", None, "tm"), P(), P(), P(), P()),
        check_vma=False,
    )
```

profile of v0, /device:TPU:0, one launch (start us, length us, event | category | flops | bytes accessed | tf_op | source)
XLA Modules:
  0.0 188.2 jit_solution(7671481007626582187)
XLA Ops:
  0.6 1.3 slice.296
  1.9 1.3 collective-permute-start.3
  4.1 5.5 %collective-permute-start = (f32[1,64,4]{2,1,0:T(8,128)S(1)}, f32[1,64,4]{2,1,0:T(8,128)S(1)}, u32[]{:S(2)}, u32[]{:S(2)}) collective-permute-start(f32[1,64,4]{2,1,0:T(8,128)S(1)} %get-tuple-element.15), channel_id=1, source_target_pairs={{0,1},{1,2},{2,3},{3,4},{4,5},{5,6},{6,7},{8,9},{9,10},{10,11},{11... | collective-permute-start | bytes 3080 | tf_op jit(solution)/shard_map/ppermute | solution.py:20
  9.6 1.3 collective-permute-start.1
  12.3 1.6 slice_bitcast_fusion.6
  13.9 1.2 sine_multiply_fusion.1
  15.1 9.4 %sine_multiply_fusion = (f32[1024,512]{1,0:T(8,128)S(1)}, f32[1024,512]{1,0:T(8,128)}) fusion(f32[1024]{0:T(1024)S(1)} %fusion.218, f32[1024]{0:T(1024)S(1)} %multiply_subtract_fusion), kind=kLoop, calls=%fused_computation.21 | loop fusion | flops 8388608 | bytes 4202496 | tf_op jit(solution)/shard_map/jvp()/mul | solution.py:57
  25.3 1.1 compare_select_fusion
  26.7 1.2 copy.16
  28.1 1.0 fusion.69
  29.1 1.3 convolution_add_fusion.1
  30.4 1.0 fusion.5
  31.4 1.3 compare_select_fusion.9
  32.7 1.0 convolution_reduce_fusion.2
  33.7 1.0 convolution_reduce_fusion.1
  34.7 1.0 convolution_reduce_fusion
  35.7 1.0 convolution_reduce_fusion.5
  36.7 1.0 convolution_reduce_fusion.4
  37.6 1.0 convolution_reduce_fusion.6
  38.6 1.0 convolution_reduce_fusion.3
  39.6 2.0 %multiply_reduce_fusion.6 = (f32[]{:T(128)}, f32[1,1024]{1,0:T(1,128)}, f32[1,1792]{1,0:T(1,128)S(1)}) fusion(f32[1,1024]{1,0:T(1,128)} %param.8, f32[1,1040]{1,0:T(1,128)S(1)} %squeeze.11), kind=kLoop, calls=%fused_computation.340 | loop fusion | flops 4094 | bytes 16388 | tf_op jit(solution)/shard_map/reduce_sum | solution.py:220
  42.3 1.3 collective-permute-start.2
  45.4 1.3 reduce.11
  46.7 1.3 reshape.962
  48.0 1.4 reshape.970
  51.1 4.3 %fusion.15 = f32[1,4,1024]{2,1,0:T(4,128)} fusion(f32[1024,512]{1,0:T(8,128)S(1)} %get-tuple-element.77, f32[1024,512]{1,0:T(8,128)} %get-tuple-element.78, f32[1,4,256]{2,1,0:T(4,128)S(1)} %get-tuple-element.45, f32[1,4,256]{2,1,0:T(4,128)S(1)} %get-tuple-element.46, f32[1,4,256]{2,1,0:T(4,128)S(1)} %get-tuple-element.47, ...), kind=kOutput, calls=%fused_computation.33 | convolution fusion | flops 51392512 | bytes 4227072 | tf_op jit(solution)/shard_map/...nf,fk->...nk/dot_general | solution.py:36
  55.4 0.9 convolution_bitcast_fusion.10
  56.3 1.3 maximum_reduce_fusion
  57.6 1.3 reshape.959
  58.9 1.3 fusion.210
  60.2 1.4 reshape.967
  61.6 1.4 fusion.285
  63.0 0.9 fusion.283
  63.9 1.2 convolution_bitcast_fusion.11
  65.9 0.9 fusion.20
  67.6 1.3 convolution_bitcast_fusion.9
  69.7 1.4 reshape.974
  71.7 6.2 %collective-permute-start.5 = (f32[1,768]{1,0:T(1,128)S(1)}, f32[1,768]{1,0:T(1,128)S(1)}, u32[]{:S(2)}, u32[]{:S(2)}) collective-permute-start(f32[1,768]{1,0:T(1,128)S(1)} %pad.112), channel_id=1, source_target_pairs={{0,1},{1,2},{2,3},{3,4},{4,5},{5,6},{6,7},{8,9},{9,10},{10,11},{11... | collective-permute-start | bytes 9224 | tf_op jit(solution)/shard_map/ppermute | solution.py:32
  78.0 3.7 %fusion.14 = f32[1,4,1024]{2,1,0:T(4,128)S(1)} fusion(f32[1024,512]{1,0:T(8,128)S(1)} %get-tuple-element.77, f32[1024,512]{1,0:T(8,128)} %get-tuple-element.78, f32[1,4,256]{2,1,0:T(4,128)} %get-tuple-element.49, f32[1,4,256]{2,1,0:T(4,128)} %get-tuple-element.50, f32[1,4,256]{2,1,0:T(4,128)} %get-tuple-element.51, f32[1,4,256]{2,1,0:T(4,128)} %get-tuple-element.48), kind=kOutput, calls=%fused_computation.32 | convolution fusion | flops 51392512 | bytes 4227072 | tf_op jit(solution)/shard_map/jvp(...nf,fk->...nk)/dot_general | solution.py:36
  83.3 3.5 %fusion.16 = f32[1,4,1024]{2,1,0:T(4,128)S(1)} fusion(f32[1024,512]{1,0:T(8,128)S(1)} %get-tuple-element.77, f32[1024,512]{1,0:T(8,128)S(1)} %copy-done.1, f32[1,4,512]{2,1,0:T(4,128)S(1)} %get-tuple-element.18, f32[1,4,512]{2,1,0:T(4,128)S(1)} %get-tuple-element.17), kind=kOutput, calls=%fused_computation.34 | convolution fusion | flops 51384320 | bytes 4227072 | tf_op jit(solution)/shard_map/transpose(jvp(...nf,fk->...nk))/dot_general | solution.py:36
  86.9 5.0 %collective-permute-start.4 = (f32[1,768]{1,0:T(1,128)S(1)}, f32[1,768]{1,0:T(1,128)S(1)}, u32[]{:S(2)}, u32[]{:S(2)}) collective-permute-start(f32[1,768]{1,0:T(1,128)S(1)} %slice.347), channel_id=1, source_target_pairs={{0,1},{1,2},{2,3},{3,4},{4,5},{5,6},{6,7},{8,9},{9,10},{10,11},{11... | collective-permute-start | bytes 9224 | tf_op jit(solution)/shard_map/ppermute | solution.py:32
  93.8 2.0 %pad_maximum_fusion.16 = f32[1,3]{1,0:T(1,128)S(1)} fusion(f32[1,1]{1,0:T(1,128)} %bitcast.63, f32[1,1]{1,0:T(1,128)} %bitcast.53, f32[1,1]{1,0:T(1,128)} %bitcast.43), kind=kLoop, calls=%fused_computation.344 | loop fusion | flops 6 | bytes 24 | tf_op jit(solution)/shard_map/stack | solution.py:220
  96.0 22.0 %psum.35 = f32[1,3]{1,0:T(1,128)S(1)} all-reduce(f32[1,3]{1,0:T(1,128)S(1)} %pad_maximum_fusion.16), channel_id=1, replica_groups=mesh['dp'=4,'tm'=8] {'tm'}, use_global_device_ids=true, to_apply=%region_3.4 | all-reduce | flops 3 | bytes 24 | tf_op jit(solution)/shard_map/psum | solution.py:221
  119.8 2.1 %add_bitcast_fusion.1 = f32[1,1,1024]{2,1,0:T(1,128)S(1)} fusion(f32[1,1024]{1,0:T(1,128)S(1)} %get-tuple-element.14, f32[1,1024]{1,0:T(1,128)S(1)} %get-tuple-element.12, f32[]{:T(128)} %bitcast.66, f32[]{:T(128)} %bitcast.65, f32[]{:T(128)} %bitcast.64, f32[1,1024]{1,0:T(1,128)} %param.8, f32[1,1040]{1,0:T(1,128)} %copy-done.14), kind=kLoop, calls=%fused_computation.336 | loop fusion | flops 6144 | bytes 20492 | tf_op jit(solution)/shard_map/broadcast_in_dim | solution.py:226
  122.0 1.3 collective-permute-start.7
  123.3 4.5 %collective-permute-start.6 = (f32[1,1,8]{2,1,0:T(1,128)S(1)}, f32[1,1,8]{2,1,0:T(1,128)S(1)}, u32[]{:S(2)}, u32[]{:S(2)}) collective-permute-start(f32[1,1,8]{2,1,0:T(1,128)S(1)} %get-tuple-element.62), channel_id=1, source_target_pairs={{0,1},{1,2},{2,3},{3,4},{4,5},{5,6},{6,7},{8,9},{9,10},{10,11},{11... | collective-permute-start | bytes 104 | tf_op jit(solution)/shard_map/ppermute | solution.py:20
  127.8 1.3 collective-permute-done.6
  136.8 41.8 %all-reduce.29 = (f32[4,32,64]{2,1,0:T(8,128)S(1)}, f32[3,16,32]{2,1,0:T(8,128)S(1)}, f32[32,16]{0,1:T(8,128)S(1)}, f32[7,32]{1,0:T(8,128)S(1)}) all-reduce(f32[4,32,64]{2,1,0:T(8,128)S(1)} %maximum_bitcast_fusion, f32[3,16,32]{2,1,0:T(8,128)S(1)} %maximum_bitcast_fusion.1, ...), channel_id=1, replica_groups=mesh['dp'=4,'tm'=8] {'dp','tm'}, use_global_device_ids=true, to_apply=%region_4.5 | all-reduce | flops 10464 | bytes 83712 | tf_op jit(solution)/shard_map/psum | solution.py:256
  (141 shorter events, 30.2 us)
Async XLA Ops:
  0.6 30.8 %copy-start = (f32[32,16]{0,1:T(8,128)S(1)}, f32[32,16]{0,1:T(8,128)}, u32[]{:S(2)}) copy-start(f32[32,16]{0,1:T(8,128)} %param.11) | copy-start | bytes 6148
  1.9 41.6 %collective-permute-start.3 = (f32[1,768]{1,0:T(1,128)}, f32[1,768]{1,0:T(1,128)}, u32[]{:S(2)}, u32[]{:S(2)}) collective-permute-start(f32[1,768]{1,0:T(1,128)} %slice.296), channel_id=1, source_target_pairs={{1,0},{2,1},{3,2},{4,3},{5,4},{6,5},{7,6},{9,8},{10,9},{11,10},{12... | collective-permute-start | bytes 9224 | tf_op jit(solution)/shard_map/ppermute | solution.py:32
  4.1 20.5 %collective-permute-start = (f32[1,64,4]{2,1,0:T(8,128)S(1)}, f32[1,64,4]{2,1,0:T(8,128)S(1)}, u32[]{:S(2)}, u32[]{:S(2)}) collective-permute-start(f32[1,64,4]{2,1,0:T(8,128)S(1)} %get-tuple-element.15), channel_id=1, source_target_pairs={{0,1},{1,2},{2,3},{3,4},{4,5},{5,6},{6,7},{8,9},{9,10},{10,11},{11... | collective-permute-start | bytes 3080 | tf_op jit(solution)/shard_map/ppermute | solution.py:20
  9.6 15.0 %collective-permute-start.1 = (f32[1,64,4]{2,1,0:T(8,128)S(1)}, f32[1,64,4]{2,1,0:T(8,128)S(1)}, u32[]{:S(2)}, u32[]{:S(2)}) collective-permute-start(f32[1,64,4]{2,1,0:T(8,128)S(1)} %get-tuple-element.16), channel_id=1, source_target_pairs={{1,0},{2,1},{3,2},{4,3},{5,4},{6,5},{7,6},{9,8},{10,9},{11,10},{12... | collective-permute-start | bytes 3080 | tf_op jit(solution)/shard_map/ppermute | solution.py:22
  15.1 9.5 %copy-start.7 = (f32[1,64,512]{2,1,0:T(8,128)S(1)}, f32[1,64,512]{2,1,0:T(8,128)}, u32[]{:S(2)}) copy-start(f32[1,64,512]{2,1,0:T(8,128)} %param.7) | copy-start | bytes 393220
  15.1 9.5 %copy-start.11 = (f32[4,32,64]{2,1,0:T(8,128)S(1)}, f32[4,32,64]{2,1,0:T(8,128)}, u32[]{:S(2)}) copy-start(f32[4,32,64]{2,1,0:T(8,128)} %param.9) | copy-start | bytes 98308
  24.6 0.6 copy-start.17
  24.6 0.6 copy-start.19
  25.3 1.1 copy-start.4
  28.0 2.4 %copy-start.6 = (f32[1,32,1040]{2,1,0:T(8,128)}, f32[1,32,1040]{2,1,0:T(8,128)S(1)}, u32[]{:S(2)}) copy-start(f32[1,32,1040]{2,1,0:T(8,128)S(1)} %copy.17) | copy-start | bytes 399364
  32.7 5.9 %copy-start.9 = (f32[1,32,1040]{2,1,0:T(8,128)}, f32[1,32,1040]{2,1,0:T(8,128)S(1)}, u32[]{:S(2)}) copy-start(f32[1,32,1040]{2,1,0:T(8,128)S(1)} %get-tuple-element.74) | copy-start | bytes 399364
  39.6 2.0 %copy-start.14 = (f32[1,1040]{1,0:T(1,128)}, f32[1,1040]{1,0:T(1,128)S(1)}, u32[]{:S(2)}) copy-start(f32[1,1040]{1,0:T(1,128)S(1)} %squeeze.11) | copy-start | bytes 12484
  42.3 14.1 %collective-permute-start.2 = (f32[1,768]{1,0:T(1,128)}, f32[1,768]{1,0:T(1,128)}, u32[]{:S(2)}, u32[]{:S(2)}) collective-permute-start(f32[1,768]{1,0:T(1,128)} %slice.333), channel_id=1, source_target_pairs={{1,0},{2,1},{3,2},{4,3},{5,4},{6,5},{7,6},{9,8},{10,9},{11,10},{12... | collective-permute-start | bytes 9224 | tf_op jit(solution)/shard_map/ppermute | solution.py:32
  44.2 0.6 copy-start.15
  51.1 4.3 %copy-start.2 = (f32[256,128]{1,0:T(8,128)S(1)}, f32[256,128]{1,0:T(8,128)}, u32[]{:S(2)}) copy-start(f32[256,128]{1,0:T(8,128)} %get-tuple-element.75) | copy-start | bytes 393220
  51.1 4.3 %copy-start.3 = (f32[256,128]{1,0:T(8,128)S(1)}, f32[256,128]{1,0:T(8,128)}, u32[]{:S(2)}) copy-start(f32[256,128]{1,0:T(8,128)} %get-tuple-element.76) | copy-start | bytes 393220
  51.1 5.2 %copy-start.16 = (f32[1,1024]{1,0:T(1,128)S(1)}, f32[1,1024]{1,0:T(1,128)}, u32[]{:S(2)}) copy-start(f32[1,1024]{1,0:T(1,128)} %get-tuple-element.53) | copy-start | bytes 12292
  71.7 20.1 %collective-permute-start.5 = (f32[1,768]{1,0:T(1,128)S(1)}, f32[1,768]{1,0:T(1,128)S(1)}, u32[]{:S(2)}, u32[]{:S(2)}) collective-permute-start(f32[1,768]{1,0:T(1,128)S(1)} %pad.112), channel_id=1, source_target_pairs={{0,1},{1,2},{2,3},{3,4},{4,5},{5,6},{6,7},{8,9},{9,10},{10,11},{11... | collective-permute-start | bytes 9224 | tf_op jit(solution)/shard_map/ppermute | solution.py:32
  78.0 3.7 %copy-start.23 = (f32[64]{0:T(128)S(1)}, f32[64]{0:T(128)}, u32[]{:S(2)}) copy-start(f32[64]{0:T(128)} %get-tuple-element.67) | copy-start | bytes 772
  78.0 3.7 %copy-start.24 = (f32[64]{0:T(128)S(1)}, f32[64]{0:T(128)}, u32[]{:S(2)}) copy-start(f32[64]{0:T(128)} %get-tuple-element.68) | copy-start | bytes 772
  78.0 4.1 %copy-start.22 = (f32[1,4,1024]{2,1,0:T(4,128)S(1)}, f32[1,4,1024]{2,1,0:T(4,128)}, u32[]{:S(2)}) copy-start(f32[1,4,1024]{2,1,0:T(4,128)} %fusion.15) | copy-start | bytes 49156
  81.7 1.6 copy-start.1
  83.3 8.6 %copy-start.21 = (f32[1,1216]{1,0:T(1,128)S(1)}, f32[1,1216]{1,0:T(1,128)}, u32[]{:S(2)}) copy-start(f32[1,1216]{1,0:T(1,128)} %reshape.974) | copy-start | bytes 14596
  86.8 43.6 %copy-start.10 = (f32[1,32,1040]{2,1,0:T(8,128)S(1)}, f32[1,32,1040]{2,1,0:T(8,128)}, u32[]{:S(2)}) copy-start(f32[1,32,1040]{2,1,0:T(8,128)} %copy-done.9) | copy-start | bytes 399364
  86.9 6.3 %collective-permute-start.4 = (f32[1,768]{1,0:T(1,128)S(1)}, f32[1,768]{1,0:T(1,128)S(1)}, u32[]{:S(2)}, u32[]{:S(2)}) collective-permute-start(f32[1,768]{1,0:T(1,128)S(1)} %slice.347), channel_id=1, source_target_pairs={{0,1},{1,2},{2,3},{3,4},{4,5},{5,6},{6,7},{8,9},{9,10},{10,11},{11... | collective-permute-start | bytes 9224 | tf_op jit(solution)/shard_map/ppermute | solution.py:32
  122.0 5.8 %collective-permute-start.7 = (f32[1,1,8]{2,1,0:T(1,128)S(1)}, f32[1,1,8]{2,1,0:T(1,128)S(1)}, u32[]{:S(2)}, u32[]{:S(2)}) collective-permute-start(f32[1,1,8]{2,1,0:T(1,128)S(1)} %get-tuple-element.61), channel_id=1, source_target_pairs={{1,0},{2,1},{3,2},{4,3},{5,4},{6,5},{7,6},{9,8},{10,9},{11,10},{12... | collective-permute-start | bytes 104 | tf_op jit(solution)/shard_map/ppermute | solution.py:22
  123.3 5.8 %collective-permute-start.6 = (f32[1,1,8]{2,1,0:T(1,128)S(1)}, f32[1,1,8]{2,1,0:T(1,128)S(1)}, u32[]{:S(2)}, u32[]{:S(2)}) collective-permute-start(f32[1,1,8]{2,1,0:T(1,128)S(1)} %get-tuple-element.62), channel_id=1, source_target_pairs={{0,1},{1,2},{2,3},{3,4},{4,5},{5,6},{6,7},{8,9},{9,10},{10,11},{11... | collective-permute-start | bytes 104 | tf_op jit(solution)/shard_map/ppermute | solution.py:20
  129.2 3.1 %copy-start.13 = (f32[3,16,32]{2,1,0:T(8,128)S(1)}, f32[3,16,32]{2,1,0:T(8,128)}, u32[]{:S(2)}) copy-start(f32[3,16,32]{2,1,0:T(8,128)} %param.10) | copy-start | bytes 18436
  131.2 2.7 %copy-start.5 = (f32[1,64,519]{2,1,0:T(8,128)S(1)}, f32[1,64,519]{2,1,0:T(8,128)}, u32[]{:S(2)}) copy-start(f32[1,64,519]{2,1,0:T(8,128)} %copy-done.4) | copy-start | bytes 398596
  131.7 2.7 %copy-start.8 = (f32[1,64,512]{2,1,0:T(8,128)S(1)}, f32[1,64,512]{2,1,0:T(8,128)}, u32[]{:S(2)}) copy-start(f32[1,64,512]{2,1,0:T(8,128)} %param.7) | copy-start | bytes 393220
  131.7 2.7 %copy-start.18 = (f32[1,64,4]{2,1,0:T(8,128)S(1)}, f32[1,64,4]{2,1,0:T(8,128)}, u32[]{:S(2)}) copy-start(f32[1,64,4]{2,1,0:T(8,128)} %copy-done.17) | copy-start | bytes 3076
  131.7 2.7 %copy-start.20 = (f32[1,64,4]{2,1,0:T(8,128)S(1)}, f32[1,64,4]{2,1,0:T(8,128)}, u32[]{:S(2)}) copy-start(f32[1,64,4]{2,1,0:T(8,128)} %copy-done.19) | copy-start | bytes 3076
  134.0 52.6 %copy-start.12 = (f32[4,32,64]{2,1,0:T(8,128)S(1)}, f32[4,32,64]{2,1,0:T(8,128)}, u32[]{:S(2)}) copy-start(f32[4,32,64]{2,1,0:T(8,128)} %param.9) | copy-start | bytes 98308
where the time goes:
time: 190 us; the launch traced here: 188 us
  blocking collectives  63.8 us (34%)
  matrix products  37.6 us (20%)
  other arithmetic  31.8 us (17%)
  starting transfers between devices  26.4 us (14%)
  local copies, waits for them, and re-layouts  22 us (12%)
  between operations  4.65 us (2%)
  waiting for transfers between devices  1.95 us (1%)
    psum x1, blocking collectives, local(): lax.psum((local_totals[0], local_totals[1], local_totals[2], local_totals...  41.8 us
    dot_general x44, matrix products, product(): jnp.einsum(form, left, right, precision=lax.Precision.HIGHEST, preferred_...  37.6 us
    psum x1, blocking collectives, local(): squares = lax.psum(squares, 'tm')  22 us
    ppermute x4, starting transfers between devices, from_behind(): return lax.ppermute(x, axis, pairs)  13.8 us
    mul x2, other arithmetic, dft_table(): -hann_taper * jnp.sin(angles)  10.7 us
    ppermute x2, starting transfers between devices, padded_2(): lax.ppermute(tail, axis, [(i, (i + 1) % count) for i in range(ends)])  10.1 us
    reshape x5, local copies, waits for them, and re-layouts, framed(): blocks = signal.reshape(signal.shape[:-1] + (frame_count + 3, hop_size))  6.68 us
    slice x4, local copies, waits for them, and re-layouts, framed(): blocks[..., offset:offset + frame_count, :]  4.01 us
  transfers between devices with their start and end apart: 8, of which 2 were waited for; matrix products, arithmetic and copies ran while one was open for 28% of the time, Pallas kernels for 0%

commit v1 on v0

--- a/solution.py
+++ b/solution.py
@@ -218,7 +218,9 @@
     gradients[1] = gradients[1] + jnp.pad(coarse_in, ((0, 0), (0, samples - tail_length)))
     gradients[2] = gradients[2] + jnp.pad(fine_in, ((0, 0), (0, samples - tail_length)))
     squares = jnp.stack([jnp.sum(member * member, axis=1) for member in gradients], axis=1)
-    squares = lax.psum(squares, "tm")
+    squares = squares
+    for hop in (1, 2, 4):
+        squares = squares + lax.ppermute(squares, "tm", [(dev, dev ^ hop) for dev in range(8)])
     total_samples = samples * lax.axis_size("tm")
     grad_scale = jnp.asarray(LOSS_WEIGHTS, jnp.float32)[None, :] / jnp.sqrt(
         squares / total_samples + 1e-06

time: 190 us -> 164 us (0.86)
  blocking collectives: 63.8 us -> 42.9 us
  local copies, waits for them, and re-layouts: 22 us -> 10.8 us
  starting transfers between devices: 26.4 us -> 35.1 us
  matrix products: 37.6 us -> 31.9 us
  waiting for transfers between devices: 1.95 us -> 6.63 us
    psum x1 -> x0, blocking collectives: 22 us -> none  [local(): squares = lax.psum(squares, 'tm')]
    ppermute x0 -> x3, starting transfers between devices: none -> 8.8 us  [local(): lax.ppermute(squares, 'tm', [(dev, dev ^ hop) for dev in range(8)])]
    reshape x5, local copies, waits for them, and re-layouts: 6.68 us -> 0.23 us  [framed(): blocks = signal.reshape(signal.shape[:-1] + (frame_count + 3, hop_size))]
    dot_general x44, matrix products: 37.6 us -> 31.9 us  [product(): jnp.einsum(form, left, right, precision=lax.Precision.HIGHEST, preferred_...]
    ppermute x0 -> x3, waiting for transfers between devices: none -> 4.65 us  [local(): lax.ppermute(squares, 'tm', [(dev, dev ^ hop) for dev in range(8)])]
    add x0 -> x2, other arithmetic: none -> 4.11 us  [local(): squares + lax.ppermute(squares, 'tm', [(dev, dev ^ hop) for dev in range(...]
    slice x4, local copies, waits for them, and re-layouts: 4.01 us -> 0.02 us  [framed(): blocks[..., offset:offset + frame_count, :]]
  transfers between devices with their start and end apart: 8 -> 11, of which waited for: 2 -> 5; matrix products, arithmetic and copies ran while one was open for 28% -> 29% of each run, Pallas kernels for 0% -> 0%
where the time goes in v1:
time: 164 us; the launch traced here: 163 us
  blocking collectives  42.9 us (26%)
  starting transfers between devices  35.1 us (21%)
  matrix products  31.9 us (19%)
  other arithmetic  30.4 us (19%)
  local copies, waits for them, and re-layouts  10.8 us (7%)
  waiting for transfers between devices  6.63 us (4%)
  between operations  4.92 us (3%)
    psum x1, blocking collectives, local(): lax.psum((local_totals[0], local_totals[1], local_totals[2], local_totals...  42.9 us
    dot_general x44, matrix products, product(): jnp.einsum(form, left, right, precision=lax.Precision.HIGHEST, preferred_...  31.9 us
    ppermute x4, starting transfers between devices, from_behind(): return lax.ppermute(x, axis, pairs)  13.6 us
    mul x2, other arithmetic, dft_table(): -hann_taper * jnp.sin(angles)  10.7 us
    ppermute x2, starting transfers between devices, padded_2(): lax.ppermute(tail, axis, [(i, (i + 1) % count) for i in range(ends)])  10.1 us
    ppermute x3, starting transfers between devices, local(): lax.ppermute(squares, 'tm', [(dev, dev ^ hop) for dev in range(8)])  8.8 us
    ppermute x3, waiting for transfers between devices, local(): lax.ppermute(squares, 'tm', [(dev, dev ^ hop) for dev in range(8)])  4.65 us
    add x2, other arithmetic, local(): squares + lax.ppermute(squares, 'tm', [(dev, dev ^ hop) for dev in range(...  4.11 us
  transfers between devices with their start and end apart: 11, of which 5 were waited for; matrix products, arithmetic and copies ran while one was open for 29% of the time, Pallas kernels for 0%

profile of v1, /device:TPU:0, one launch (start us, length us, event | category | flops | bytes accessed | tf_op | source)
XLA Modules:
  0.0 162.6 jit_solution(8714940235279228507)
XLA Ops:
  0.6 1.3 slice.296
  1.9 1.3 collective-permute-start.3
  3.2 0.9 fusion.279
  4.1 5.5 %collective-permute-start = (f32[1,64,4]{2,1,0:T(8,128)S(1)}, f32[1,64,4]{2,1,0:T(8,128)S(1)}, u32[]{:S(2)}, u32[]{:S(2)}) collective-permute-start(f32[1,64,4]{2,1,0:T(8,128)S(1)} %get-tuple-element.15), channel_id=1, source_target_pairs={{0,1},{1,2},{2,3},{3,4},{4,5},{5,6},{6,7},{8,9},{9,10},{10,11},{11... | collective-permute-start | bytes 3080 | tf_op jit(solution)/shard_map/ppermute | solution.py:20
  9.6 1.3 collective-permute-start.1
  11.7 0.7 fusion.288
  12.4 1.5 slice_bitcast_fusion.6
  13.9 1.2 sine_multiply_fusion.1
  15.2 9.4 %sine_multiply_fusion = (f32[1024,512]{1,0:T(8,128)S(1)}, f32[1024,512]{1,0:T(8,128)}) fusion(f32[1024]{0:T(1024)S(1)} %fusion.218, f32[1024]{0:T(1024)S(1)} %multiply_subtract_fusion), kind=kLoop, calls=%fused_computation.21 | loop fusion | flops 8388608 | bytes 4202496 | tf_op jit(solution)/shard_map/jvp()/mul | solution.py:57
  26.7 1.0 fusion.69
  27.7 1.3 convolution_add_fusion.1
  29.0 1.0 fusion.5
  30.0 1.3 compare_select_fusion.9
  31.3 1.0 convolution_reduce_fusion.2
  32.3 1.0 convolution_reduce_fusion.1
  33.3 1.0 convolution_reduce_fusion
  34.3 1.0 convolution_reduce_fusion.5
  35.3 1.0 convolution_reduce_fusion.4
  36.2 1.0 convolution_reduce_fusion.6
  37.2 1.0 convolution_reduce_fusion.3
  38.2 2.0 %multiply_reduce_fusion.6 = (f32[]{:T(128)}, f32[1,1024]{1,0:T(1,128)}, f32[1,1792]{1,0:T(1,128)}) fusion(f32[1,1024]{1,0:T(1,128)} %param.8, f32[1,1040]{1,0:T(1,128)S(1)} %squeeze.11), kind=kLoop, calls=%fused_computation.340 | loop fusion | flops 4094 | bytes 16896 | tf_op jit(solution)/shard_map/reduce_sum | solution.py:220
  40.3 0.7 slice.333
  40.9 0.9 copy.20
  41.8 1.3 collective-permute-start.2
  43.1 1.3 constant_dynamic-update-slice_fusion
  44.3 0.7 slice_reduce_fusion
  45.1 0.7 reduce.11
  45.9 3.8 %fusion.15 = f32[1,4,1024]{2,1,0:T(4,128)S(1)} fusion(f32[1024,512]{1,0:T(8,128)S(1)} %get-tuple-element.77, f32[1024,512]{1,0:T(8,128)} %get-tuple-element.78, f32[1,4,256]{2,1,0:T(4,128)S(1)} %get-tuple-element.45, f32[1,4,256]{2,1,0:T(4,128)S(1)} %get-tuple-element.46, f32[1,4,256]{2,1,0:T(4,128)S(1)} %get-tuple-element.47, ...), kind=kOutput, calls=%fused_computation.33 | convolution fusion | flops 51392512 | bytes 4227072 | tf_op jit(solution)/shard_map/...nf,fk->...nk/dot_general | solution.py:36
  51.6 6.3 %collective-permute-start.5 = (f32[1,768]{1,0:T(1,128)S(1)}, f32[1,768]{1,0:T(1,128)S(1)}, u32[]{:S(2)}, u32[]{:S(2)}) collective-permute-start(f32[1,768]{1,0:T(1,128)S(1)} %pad.112), channel_id=1, source_target_pairs={{0,1},{1,2},{2,3},{3,4},{4,5},{5,6},{6,7},{8,9},{9,10},{10,11},{11... | collective-permute-start | bytes 9224 | tf_op jit(solution)/shard_map/ppermute | solution.py:32
  57.9 3.7 %fusion.14 = f32[1,4,1024]{2,1,0:T(4,128)S(1)} fusion(f32[1024,512]{1,0:T(8,128)S(1)} %get-tuple-element.77, f32[1024,512]{1,0:T(8,128)} %get-tuple-element.78, f32[1,4,256]{2,1,0:T(4,128)S(1)} %get-tuple-element.49, f32[1,4,256]{2,1,0:T(4,128)S(1)} %get-tuple-element.50, f32[1,4,256]{2,1,0:T(4,128)S(1)} %get-tuple-element.51, ...), kind=kOutput, calls=%fused_computation.32 | convolution fusion | flops 51392512 | bytes 4227072 | tf_op jit(solution)/shard_map/jvp(...nf,fk->...nk)/dot_general | solution.py:36
  63.2 3.5 %fusion.16 = f32[1,4,1024]{2,1,0:T(4,128)S(1)} fusion(f32[1024,512]{1,0:T(8,128)S(1)} %get-tuple-element.77, f32[1024,512]{1,0:T(8,128)S(1)} %copy-done.1, f32[1,4,512]{2,1,0:T(4,128)S(1)} %get-tuple-element.18, f32[1,4,512]{2,1,0:T(4,128)S(1)} %get-tuple-element.17), kind=kOutput, calls=%fused_computation.34 | convolution fusion | flops 51384320 | bytes 4227072 | tf_op jit(solution)/shard_map/transpose(jvp(...nf,fk->...nk))/dot_general | solution.py:36
  66.8 4.8 %collective-permute-start.4 = (f32[1,768]{1,0:T(1,128)S(1)}, f32[1,768]{1,0:T(1,128)S(1)}, u32[]{:S(2)}, u32[]{:S(2)}) collective-permute-start(f32[1,768]{1,0:T(1,128)S(1)} %slice.347), channel_id=1, source_target_pairs={{0,1},{1,2},{2,3},{3,4},{4,5},{5,6},{6,7},{8,9},{9,10},{10,11},{11... | collective-permute-start | bytes 9224 | tf_op jit(solution)/shard_map/ppermute | solution.py:32
  72.3 0.7 collective-permute-done.4
  73.6 2.1 %pad_maximum_fusion.16 = f32[1,3]{1,0:T(1,128)S(1)} fusion(f32[1,1]{1,0:T(1,128)} %bitcast.63, f32[1,1]{1,0:T(1,128)} %bitcast.53, f32[1,1]{1,0:T(1,128)} %bitcast.43), kind=kLoop, calls=%fused_computation.344 | loop fusion | flops 6 | bytes 24 | tf_op jit(solution)/shard_map/stack | solution.py:220
  75.6 2.3 %collective-permute-start.6 = (f32[1,3]{1,0:T(1,128)S(1)}, f32[1,3]{1,0:T(1,128)S(1)}, u32[]{:S(2)}, u32[]{:S(2)}) collective-permute-start(f32[1,3]{1,0:T(1,128)S(1)} %pad_maximum_fusion.16), channel_id=1, source_target_pairs={{0,1},{1,0},{2,3},{3,2},{4,5},{5,4},{6,7},{7,6},{8,9},{9,8},{10,11... | collective-permute-start | bytes 44 | tf_op jit(solution)/shard_map/ppermute | solution.py:223
  77.9 1.5 collective-permute-done.6
  79.4 2.1 %fusion.300 = f32[1,3]{1,0:T(1,128)S(1)} fusion(f32[1,3]{1,0:T(1,128)S(1)} %collective-permute-done.6, f32[1,1]{1,0:T(1,128)} %bitcast.63, f32[1,1]{1,0:T(1,128)} %bitcast.53, f32[1,1]{1,0:T(1,128)} %bitcast.43), kind=kLoop, calls=%fused_computation.429 | loop fusion | flops 9 | bytes 36 | tf_op jit(solution)/shard_map/add | solution.py:223
  81.5 3.5 %collective-permute-start.7 = (f32[1,3]{1,0:T(1,128)S(1)}, f32[1,3]{1,0:T(1,128)S(1)}, u32[]{:S(2)}, u32[]{:S(2)}) collective-permute-start(f32[1,3]{1,0:T(1,128)S(1)} %fusion.300), channel_id=1, source_target_pairs={{0,2},{1,3},{2,0},{3,1},{4,6},{5,7},{6,4},{7,5},{8,10},{9,11},{10,... | collective-permute-start | bytes 44 | tf_op jit(solution)/shard_map/ppermute | solution.py:223
  85.0 1.5 collective-permute-done.7
  86.5 2.1 %fusion.301 = f32[1,3]{1,0:T(1,128)S(1)} fusion(f32[1,3]{1,0:T(1,128)S(1)} %collective-permute-done.7, f32[1,3]{1,0:T(1,128)S(1)} %collective-permute-done.6, f32[1,1]{1,0:T(1,128)} %bitcast.63, f32[1,1]{1,0:T(1,128)} %bitcast.53, f32[1,1]{1,0:T(1,128)} %bitcast.43), kind=kLoop, calls=%fused_computation.430 | loop fusion | flops 12 | bytes 48 | tf_op jit(solution)/shard_map/add | solution.py:223
  88.6 3.0 %collective-permute-start.8 = (f32[1,3]{1,0:T(1,128)S(1)}, f32[1,3]{1,0:T(1,128)S(1)}, u32[]{:S(2)}, u32[]{:S(2)}) collective-permute-start(f32[1,3]{1,0:T(1,128)S(1)} %fusion.301), channel_id=1, source_target_pairs={{0,4},{1,5},{2,6},{3,7},{4,0},{5,1},{6,2},{7,3},{8,12},{9,13},{10,... | collective-permute-start | bytes 44 | tf_op jit(solution)/shard_map/ppermute | solution.py:223
  91.6 1.5 collective-permute-done.8
  94.5 1.4 add_bitcast_fusion.1
  95.9 1.3 collective-permute-start.10
  97.2 4.5 %collective-permute-start.9 = (f32[1,1,8]{2,1,0:T(1,128)S(1)}, f32[1,1,8]{2,1,0:T(1,128)S(1)}, u32[]{:S(2)}, u32[]{:S(2)}) collective-permute-start(f32[1,1,8]{2,1,0:T(1,128)S(1)} %get-tuple-element.62), channel_id=1, source_target_pairs={{0,1},{1,2},{2,3},{3,4},{4,5},{5,6},{6,7},{8,9},{9,10},{10,11},{11... | collective-permute-start | bytes 104 | tf_op jit(solution)/shard_map/ppermute | solution.py:20
  101.8 1.3 collective-permute-done.9
  110.1 42.9 %all-reduce.29 = (f32[4,32,64]{2,1,0:T(8,128)S(1)}, f32[3,16,32]{2,1,0:T(8,128)S(1)}, f32[32,16]{0,1:T(8,128)S(1)}, f32[7,32]{1,0:T(8,128)S(1)}) all-reduce(f32[4,32,64]{2,1,0:T(8,128)S(1)} %maximum_bitcast_fusion, f32[3,16,32]{2,1,0:T(8,128)S(1)} %maximum_bitcast_fusion.1, ...), channel_id=1, replica_groups=mesh['dp'=4,'tm'=8] {'dp','tm'}, use_global_device_ids=true, to_apply=%region_3.4 | all-reduce | flops 10464 | bytes 83712 | tf_op jit(solution)/shard_map/psum | solution.py:258
  161.8 0.8 fusion.92
  (168 shorter events, 21.2 us)
Async XLA Ops:
  0.6 29.4 %copy-start = (f32[32,16]{0,1:T(8,128)S(1)}, f32[32,16]{0,1:T(8,128)}, u32[]{:S(2)}) copy-start(f32[32,16]{0,1:T(8,128)} %param.11) | copy-start | bytes 6148
  1.9 41.1 %collective-permute-start.3 = (f32[1,768]{1,0:T(1,128)}, f32[1,768]{1,0:T(1,128)}, u32[]{:S(2)}, u32[]{:S(2)}) collective-permute-start(f32[1,768]{1,0:T(1,128)} %slice.296), channel_id=1, source_target_pairs={{1,0},{2,1},{3,2},{4,3},{5,4},{6,5},{7,6},{9,8},{10,9},{11,10},{12... | collective-permute-start | bytes 9224 | tf_op jit(solution)/shard_map/ppermute | solution.py:32
  4.1 20.6 %collective-permute-start = (f32[1,64,4]{2,1,0:T(8,128)S(1)}, f32[1,64,4]{2,1,0:T(8,128)S(1)}, u32[]{:S(2)}, u32[]{:S(2)}) collective-permute-start(f32[1,64,4]{2,1,0:T(8,128)S(1)} %get-tuple-element.15), channel_id=1, source_target_pairs={{0,1},{1,2},{2,3},{3,4},{4,5},{5,6},{6,7},{8,9},{9,10},{10,11},{11... | collective-permute-start | bytes 3080 | tf_op jit(solution)/shard_map/ppermute | solution.py:20
  9.6 15.1 %collective-permute-start.1 = (f32[1,64,4]{2,1,0:T(8,128)S(1)}, f32[1,64,4]{2,1,0:T(8,128)S(1)}, u32[]{:S(2)}, u32[]{:S(2)}) collective-permute-start(f32[1,64,4]{2,1,0:T(8,128)S(1)} %get-tuple-element.16), channel_id=1, source_target_pairs={{1,0},{2,1},{3,2},{4,3},{5,4},{6,5},{7,6},{9,8},{10,9},{11,10},{12... | collective-permute-start | bytes 3080 | tf_op jit(solution)/shard_map/ppermute | solution.py:22
  15.2 9.5 %copy-start.7 = (f32[1,64,512]{2,1,0:T(8,128)S(1)}, f32[1,64,512]{2,1,0:T(8,128)}, u32[]{:S(2)}) copy-start(f32[1,64,512]{2,1,0:T(8,128)} %param.7) | copy-start | bytes 393220
  15.2 9.5 %copy-start.12 = (f32[4,32,64]{2,1,0:T(8,128)S(1)}, f32[4,32,64]{2,1,0:T(8,128)}, u32[]{:S(2)}) copy-start(f32[4,32,64]{2,1,0:T(8,128)} %param.9) | copy-start | bytes 98308
  24.7 1.1 copy-start.18
  24.7 1.1 copy-start.20
  25.3 0.7 copy-start.4
  26.6 2.4 %copy-start.6 = (f32[1,32,1040]{2,1,0:T(8,128)}, f32[1,32,1040]{2,1,0:T(8,128)S(1)}, u32[]{:S(2)}) copy-start(f32[1,32,1040]{2,1,0:T(8,128)S(1)} %copy.17) | copy-start | bytes 399364
  31.3 5.9 %copy-start.9 = (f32[1,32,1040]{2,1,0:T(8,128)}, f32[1,32,1040]{2,1,0:T(8,128)S(1)}, u32[]{:S(2)}) copy-start(f32[1,32,1040]{2,1,0:T(8,128)S(1)} %get-tuple-element.74) | copy-start | bytes 399364
  38.2 2.0 %copy-start.15 = (f32[1,1040]{1,0:T(1,128)}, f32[1,1040]{1,0:T(1,128)S(1)}, u32[]{:S(2)}) copy-start(f32[1,1040]{1,0:T(1,128)S(1)} %squeeze.11) | copy-start | bytes 12484
  41.8 8.2 %collective-permute-start.2 = (f32[1,768]{1,0:T(1,128)}, f32[1,768]{1,0:T(1,128)S(1)}, u32[]{:S(2)}, u32[]{:S(2)}) collective-permute-start(f32[1,768]{1,0:T(1,128)} %slice.333), channel_id=1, source_target_pairs={{1,0},{2,1},{3,2},{4,3},{5,4},{6,5},{7,6},{9,8},{10,9},{11,10},{12... | collective-permute-start | bytes 9224 | tf_op jit(solution)/shard_map/ppermute | solution.py:32
  45.9 3.8 %copy-start.2 = (f32[256,128]{1,0:T(8,128)S(1)}, f32[256,128]{1,0:T(8,128)}, u32[]{:S(2)}) copy-start(f32[256,128]{1,0:T(8,128)} %get-tuple-element.75) | copy-start | bytes 393220
  45.9 3.8 %copy-start.3 = (f32[256,128]{1,0:T(8,128)S(1)}, f32[256,128]{1,0:T(8,128)}, u32[]{:S(2)}) copy-start(f32[256,128]{1,0:T(8,128)} %get-tuple-element.76) | copy-start | bytes 393220
  45.9 4.1 %copy-start.17 = (f32[1,1024]{1,0:T(1,128)S(1)}, f32[1,1024]{1,0:T(1,128)}, u32[]{:S(2)}) copy-start(f32[1,1024]{1,0:T(1,128)} %get-tuple-element.53) | copy-start | bytes 12292
  45.9 4.5 %copy-start.33 = (f32[64]{0:T(128)S(1)}, f32[64]{0:T(128)}, u32[]{:S(2)}) copy-start(f32[64]{0:T(128)} %get-tuple-element.69) | copy-start | bytes 772
  45.9 4.5 %copy-start.34 = (f32[64]{0:T(128)S(1)}, f32[64]{0:T(128)}, u32[]{:S(2)}) copy-start(f32[64]{0:T(128)} %get-tuple-element.70) | copy-start | bytes 772
  51.6 20.1 %collective-permute-start.5 = (f32[1,768]{1,0:T(1,128)S(1)}, f32[1,768]{1,0:T(1,128)S(1)}, u32[]{:S(2)}, u32[]{:S(2)}) collective-permute-start(f32[1,768]{1,0:T(1,128)S(1)} %pad.112), channel_id=1, source_target_pairs={{0,1},{1,2},{2,3},{3,4},{4,5},{5,6},{6,7},{8,9},{9,10},{10,11},{11... | collective-permute-start | bytes 9224 | tf_op jit(solution)/shard_map/ppermute | solution.py:32
  57.8 3.7 %copy-start.31 = (f32[64]{0:T(128)S(1)}, f32[64]{0:T(128)}, u32[]{:S(2)}) copy-start(f32[64]{0:T(128)} %get-tuple-element.67) | copy-start | bytes 772
  57.9 3.7 %copy-start.32 = (f32[64]{0:T(128)S(1)}, f32[64]{0:T(128)}, u32[]{:S(2)}) copy-start(f32[64]{0:T(128)} %get-tuple-element.68) | copy-start | bytes 772
  61.5 1.6 copy-start.1
  63.1 30.0 %copy-start.30 = (f32[1,3]{1,0:T(1,128)S(1)}, f32[1,3]{1,0:T(1,128)}, u32[]{:S(2)}) copy-start(f32[1,3]{1,0:T(1,128)} %constant.211) | copy-start | bytes 40
  63.1 31.3 %copy-start.16 = (f32[1,1040]{1,0:T(1,128)S(1)}, f32[1,1040]{1,0:T(1,128)}, u32[]{:S(2)}) copy-start(f32[1,1040]{1,0:T(1,128)} %copy-done.15) | copy-start | bytes 12484
  63.1 31.3 %copy-start.22 = (f32[1,1024]{1,0:T(1,128)S(1)}, f32[1,1024]{1,0:T(1,128)}, u32[]{:S(2)}) copy-start(f32[1,1024]{1,0:T(1,128)} %param.8) | copy-start | bytes 12292
  63.1 40.3 %copy-start.23 = (f32[32]{0:T(128)S(1)}, f32[32]{0:T(128)}, u32[]{:S(2)}) copy-start(f32[32]{0:T(128)} %get-tuple-element.54) | copy-start | bytes 388
  63.1 40.4 %copy-start.24 = (f32[32]{0:T(128)S(1)}, f32[32]{0:T(128)}, u32[]{:S(2)}) copy-start(f32[32]{0:T(128)} %get-tuple-element.55) | copy-start | bytes 388
  63.2 40.4 %copy-start.25 = (f32[32]{0:T(128)S(1)}, f32[32]{0:T(128)}, u32[]{:S(2)}) copy-start(f32[32]{0:T(128)} %get-tuple-element.56) | copy-start | bytes 388
  63.2 40.4 %copy-start.26 = (f32[32]{0:T(128)S(1)}, f32[32]{0:T(128)}, u32[]{:S(2)}) copy-start(f32[32]{0:T(128)} %get-tuple-element.57) | copy-start | bytes 388
  63.2 40.4 %copy-start.27 = (f32[32]{0:T(128)S(1)}, f32[32]{0:T(128)}, u32[]{:S(2)}) copy-start(f32[32]{0:T(128)} %get-tuple-element.58) | copy-start | bytes 388
  63.2 40.4 %copy-start.28 = (f32[32]{0:T(128)S(1)}, f32[32]{0:T(128)}, u32[]{:S(2)}) copy-start(f32[32]{0:T(128)} %get-tuple-element.59) | copy-start | bytes 388
  63.2 40.4 %copy-start.29 = (f32[32]{0:T(128)S(1)}, f32[32]{0:T(128)}, u32[]{:S(2)}) copy-start(f32[32]{0:T(128)} %get-tuple-element.60) | copy-start | bytes 388
  63.2 40.5 %copy-start.10 = (f32[1,32,1040]{2,1,0:T(8,128)S(1)}, f32[1,32,1040]{2,1,0:T(8,128)}, u32[]{:S(2)}) copy-start(f32[1,32,1040]{2,1,0:T(8,128)} %copy-done.9) | copy-start | bytes 399364
  66.8 6.1 %collective-permute-start.4 = (f32[1,768]{1,0:T(1,128)S(1)}, f32[1,768]{1,0:T(1,128)S(1)}, u32[]{:S(2)}, u32[]{:S(2)}) collective-permute-start(f32[1,768]{1,0:T(1,128)S(1)} %slice.347), channel_id=1, source_target_pairs={{0,1},{1,2},{2,3},{3,4},{4,5},{5,6},{6,7},{8,9},{9,10},{10,11},{11... | collective-permute-start | bytes 9224 | tf_op jit(solution)/shard_map/ppermute | solution.py:32
  75.6 3.8 %collective-permute-start.6 = (f32[1,3]{1,0:T(1,128)S(1)}, f32[1,3]{1,0:T(1,128)S(1)}, u32[]{:S(2)}, u32[]{:S(2)}) collective-permute-start(f32[1,3]{1,0:T(1,128)S(1)} %pad_maximum_fusion.16), channel_id=1, source_target_pairs={{0,1},{1,0},{2,3},{3,2},{4,5},{5,4},{6,7},{7,6},{8,9},{9,8},{10,11... | collective-permute-start | bytes 44 | tf_op jit(solution)/shard_map/ppermute | solution.py:223
  81.5 5.0 %collective-permute-start.7 = (f32[1,3]{1,0:T(1,128)S(1)}, f32[1,3]{1,0:T(1,128)S(1)}, u32[]{:S(2)}, u32[]{:S(2)}) collective-permute-start(f32[1,3]{1,0:T(1,128)S(1)} %fusion.300), channel_id=1, source_target_pairs={{0,2},{1,3},{2,0},{3,1},{4,6},{5,7},{6,4},{7,5},{8,10},{9,11},{10,... | collective-permute-start | bytes 44 | tf_op jit(solution)/shard_map/ppermute | solution.py:223
  88.6 4.6 %collective-permute-start.8 = (f32[1,3]{1,0:T(1,128)S(1)}, f32[1,3]{1,0:T(1,128)S(1)}, u32[]{:S(2)}, u32[]{:S(2)}) collective-permute-start(f32[1,3]{1,0:T(1,128)S(1)} %fusion.301), channel_id=1, source_target_pairs={{0,4},{1,5},{2,6},{3,7},{4,0},{5,1},{6,2},{7,3},{8,12},{9,13},{10,... | collective-permute-start | bytes 44 | tf_op jit(solution)/shard_map/ppermute | solution.py:223
  95.9 5.8 %collective-permute-start.10 = (f32[1,1,8]{2,1,0:T(1,128)S(1)}, f32[1,1,8]{2,1,0:T(1,128)S(1)}, u32[]{:S(2)}, u32[]{:S(2)}) collective-permute-start(f32[1,1,8]{2,1,0:T(1,128)S(1)} %get-tuple-element.61), channel_id=1, source_target_pairs={{1,0},{2,1},{3,2},{4,3},{5,4},{6,5},{7,6},{9,8},{10,9},{11,10},{12... | collective-permute-start | bytes 104 | tf_op jit(solution)/shard_map/ppermute | solution.py:22
  97.2 5.8 %collective-permute-start.9 = (f32[1,1,8]{2,1,0:T(1,128)S(1)}, f32[1,1,8]{2,1,0:T(1,128)S(1)}, u32[]{:S(2)}, u32[]{:S(2)}) collective-permute-start(f32[1,1,8]{2,1,0:T(1,128)S(1)} %get-tuple-element.62), channel_id=1, source_target_pairs={{0,1},{1,2},{2,3},{3,4},{4,5},{5,6},{6,7},{8,9},{9,10},{10,11},{11... | collective-permute-start | bytes 104 | tf_op jit(solution)/shard_map/ppermute | solution.py:20
  103.1 2.5 %copy-start.14 = (f32[3,16,32]{2,1,0:T(8,128)S(1)}, f32[3,16,32]{2,1,0:T(8,128)}, u32[]{:S(2)}) copy-start(f32[3,16,32]{2,1,0:T(8,128)} %param.10) | copy-start | bytes 18436
  103.7 3.0 %copy-start.11 = (f32[1,1,32,1040]{3,2,1,0:T(8,128)S(1)}, f32[1,1,32,1040]{3,2,1,0:T(8,128)}, u32[]{:S(2)}) copy-start(f32[1,1,32,1040]{3,2,1,0:T(8,128)} %copy.20) | copy-start | bytes 399364
  104.5 2.7 %copy-start.5 = (f32[1,64,519]{2,1,0:T(8,128)S(1)}, f32[1,64,519]{2,1,0:T(8,128)}, u32[]{:S(2)}) copy-start(f32[1,64,519]{2,1,0:T(8,128)} %copy-done.4) | copy-start | bytes 398596
  104.9 2.7 %copy-start.8 = (f32[1,64,512]{2,1,0:T(8,128)S(1)}, f32[1,64,512]{2,1,0:T(8,128)}, u32[]{:S(2)}) copy-start(f32[1,64,512]{2,1,0:T(8,128)} %param.7) | copy-start | bytes 393220
  105.0 2.7 %copy-start.19 = (f32[1,64,4]{2,1,0:T(8,128)S(1)}, f32[1,64,4]{2,1,0:T(8,128)}, u32[]{:S(2)}) copy-start(f32[1,64,4]{2,1,0:T(8,128)} %copy-done.18) | copy-start | bytes 3076
  105.0 2.7 %copy-start.21 = (f32[1,64,4]{2,1,0:T(8,128)S(1)}, f32[1,64,4]{2,1,0:T(8,128)}, u32[]{:S(2)}) copy-start(f32[1,64,4]{2,1,0:T(8,128)} %copy-done.20) | copy-start | bytes 3076
  107.3 53.7 %copy-start.13 = (f32[4,32,64]{2,1,0:T(8,128)S(1)}, f32[4,32,64]{2,1,0:T(8,128)}, u32[]{:S(2)}) copy-start(f32[4,32,64]{2,1,0:T(8,128)} %param.9) | copy-start | bytes 98308
